TPU v7x, 256 devices: a whole 4x4x8 slice. The times are simulated.
256 devices in a mesh: req: 64 (over x, z, core), tensor: 4 (over y).
Axes of the slice: x: 4, y: 4, z: 8, core: 2. Of those that a mesh axis runs over, the one named last changes fastest.
Arguments:
- stream: bfloat16 [65536, 2048], P('req', 'tensor'), may hold values from -64 to 64
- target_row: int32 [65536], P('req'), may hold values from -1 to 65535, as said below
- segment_ids: int32 [65536], P('req'), may hold values from -1 to 63, as said below
- cache_slot: int32 [65536], P('req'), may hold values from -1 to 2047, as said below
- norm_gain: bfloat16 [2048], replicated, may hold values from 0.099609375 to 1.8984375
- norm_bias: bfloat16 [2048], replicated, may hold values from -3 to 3
- projection: bfloat16 [2048, 3, 2048], P(None, None, 'tensor'), may hold values from -1 to 1
- output_weight: bfloat16 [2048, 2048], P('tensor'), may hold values from -0.125 to 0.125
- cache_pool: bfloat16 [131072, 2, 2048], P('req', None, 'tensor'), may hold values from -6 to 6
Outputs:
- mixed: bfloat16 [65536, 2048], P('req', 'tensor')
- new_pool: bfloat16 [131072, 2, 2048], P('req', None, 'tensor')
Inputs may be any that keep to these rules, and one draw needn't show every extreme that they name: `target_row`: every live row of the request layout is named by exactly one stream row and no other row is named. A device names at most 16 rows of any one device; in every draw some device receives exactly 16 rows from every device and its 1024 rows are all live. `segment_ids`: within one device's 1024 rows the numbers start at 0 on the first row, rise by one at each new request and never fall; a request's rows are consecutive and never cross devices; -1 only on the rows after the last request. A device holds at most 64 requests, and in every draw some device holds exactly that many. `cache_slot`: live rows of one device have distinct slots; a request's rows fill its pages in order, each page being 16 consecutive slots beginning at a multiple of 16; -1 exactly on rows where segment_ids is -1.
All inputs are finite; a program needn't handle non-finite values.
Results may differ from a plain program's by a relative error of at most 0.008.
Values may be sent and summed in bfloat16 or wider, within the bound.
No kernel may reach another device: no remote copies, remote signals or barrier semaphores. Data moves between devices by JAX's collectives and lax.ppermute only.
A program may use at most 128 MiB of HBM per device.

v0:
```python
import math
import jax
import jax.numpy as jnp
from jax import lax
from jax.sharding import PartitionSpec as P

HDIM = 256
ROT = 64
norm_epsilon = 1e-05
masked_score = -1e30
rotary_base = 10000.0


def layer_norm(values, norm_gain, norm_bias):
    widened = values.astype(jnp.float32)
    row_mean = jnp.mean(widened, axis=-1, keepdims=True)
    centred = widened - row_mean
    row_var = jnp.mean(centred * centred, axis=-1, keepdims=True)
    scaled = centred * lax.rsqrt(row_var + norm_epsilon)
    return (scaled * norm_gain.astype(jnp.float32) + norm_bias.astype(jnp.float32)).astype(
        jnp.bfloat16
    )


def rotary(heads_in, position):
    half_rot = ROT // 2
    exponent = jnp.arange(half_rot, dtype=jnp.float32) * (2.0 / ROT)
    inverse_freq = 1.0 / rotary_base**exponent
    angles = position.astype(jnp.float32)[:, None] * inverse_freq[None, :]
    cosine = jnp.cos(angles)[:, None, :]
    sine_part = jnp.sin(angles)[:, None, :]
    widened = heads_in.astype(jnp.float32)
    row_count = widened.shape[0]
    head_count = widened.shape[1]
    paired = widened[..., :ROT].reshape(row_count, head_count, half_rot, 2)
    even_part = paired[..., 0]
    odd_part = paired[..., 1]
    turned = jnp.stack(
        [even_part * cosine - odd_part * sine_part, odd_part * cosine + even_part * sine_part],
        axis=-1,
    )
    turned = turned.reshape(row_count, head_count, ROT)
    return jnp.concatenate([turned, widened[..., ROT:]], axis=-1).astype(jnp.bfloat16)


def project(split_rows, norm_gain, norm_bias, projection):
    features_all = lax.all_gather(split_rows, "tensor", axis=1, tiled=True)
    normed = layer_norm(features_all, norm_gain, norm_bias)
    flat_weight = projection.reshape(projection.shape[0], projection.shape[1] * projection.shape[2])
    return jnp.dot(normed, flat_weight, preferred_element_type=jnp.float32).astype(jnp.bfloat16)


def masked_softmax(scores, allowed):
    scores = jnp.where(allowed[None], scores, masked_score)
    top_score = jnp.max(scores, axis=-1, keepdims=True)
    raised = jnp.where(allowed[None], jnp.exp(scores - top_score), 0.0)
    row_total = jnp.sum(raised, axis=-1, keepdims=True)
    row_total = jnp.where(row_total > 0.0, row_total, 1.0)
    return (raised / row_total).astype(jnp.bfloat16)


def source_of(wanted, labels):
    matches = labels[None, :] == wanted[:, None]
    label_ids = jnp.arange(labels.shape[0], dtype=jnp.int32)
    source = jnp.sum(jnp.where(matches, label_ids[None, :], 0), axis=1)
    return (source, jnp.any(matches, axis=1))


def shards(
    stream,
    target_row,
    segment_ids,
    cache_slot,
    norm_gain,
    norm_bias,
    projection,
    output_weight,
    cache_pool,
):
    peer_count = lax.axis_size("req")
    row_count = stream.shape[0]
    cap_rows = row_count // peer_count
    head_width = projection.shape[2]
    local_heads = head_width // HDIM
    score_scale = 1.0 / math.sqrt(HDIM)
    row_ids = jnp.arange(row_count, dtype=jnp.int32)
    sends_row = target_row >= 0
    receiver = jnp.where(sends_row, target_row // row_count, peer_count)
    local_row = jnp.where(sends_row, target_row % row_count, -1)
    onehot = (receiver[:, None] == jnp.arange(peer_count, dtype=jnp.int32)[None, :]).astype(
        jnp.bfloat16
    )
    strictly_lower = (row_ids[None, :] < row_ids[:, None]).astype(jnp.bfloat16)
    before_count = jnp.dot(strictly_lower, onehot, preferred_element_type=jnp.float32)
    slot_rank = jnp.sum(before_count * onehot.astype(jnp.float32), axis=1).astype(jnp.int32)
    send_slot = jnp.where(sends_row, receiver * cap_rows + slot_rank, -1)
    buffer_ids = jnp.arange(peer_count * cap_rows, dtype=jnp.int32)
    send_source, send_filled = source_of(buffer_ids, send_slot)
    send_rows = jnp.where(send_filled, local_row[send_source], -1).reshape(peer_count, cap_rows)

    def pack(values):
        buffer = jnp.where(
            send_filled[:, None], jnp.take(values, send_source, axis=0), jnp.zeros((), values.dtype)
        )
        return buffer.reshape(peer_count, cap_rows, values.shape[1])

    def unpack(buffer, arrived_rows):
        arrived_source, arrived_found = source_of(row_ids, arrived_rows.reshape(-1))
        flat_values = buffer.reshape(peer_count * cap_rows, buffer.shape[2])
        return jnp.where(
            arrived_found[:, None],
            jnp.take(flat_values, arrived_source, axis=0),
            jnp.zeros((), buffer.dtype),
        )

    projected = project(stream, norm_gain, norm_bias, projection)
    got_stream, got_projected, got_rows = (
        lax.all_to_all(pack(stream), "req", split_axis=0, concat_axis=0, tiled=True),
        lax.all_to_all(pack(projected), "req", split_axis=0, concat_axis=0, tiled=True),
        lax.all_to_all(send_rows, "req", split_axis=0, concat_axis=0, tiled=True),
    )
    placed = unpack(got_stream, got_rows)
    projected = unpack(got_projected, got_rows)
    is_live = segment_ids >= 0
    allowed = (segment_ids[:, None] == segment_ids[None, :]) & (
        row_ids[None, :] <= row_ids[:, None]
    )
    position = jnp.sum(allowed.astype(jnp.int32), axis=1) - 1
    projected = projected.reshape(row_count, 3, local_heads, HDIM)
    queries = rotary(projected[:, 0], position)
    keys_rot = rotary(projected[:, 1], position)
    values_all = projected[:, 2]
    scores = (
        jnp.einsum("qhd,khd->hqk", queries, keys_rot, preferred_element_type=jnp.float32)
        * score_scale
    )
    weights = masked_softmax(scores, allowed)
    context = jnp.einsum("hqk,khd->qhd", weights, values_all, preferred_element_type=jnp.float32)
    context = context.astype(jnp.bfloat16)
    head_partial = jnp.dot(
        context.reshape(row_count, head_width), output_weight, preferred_element_type=jnp.float32
    )
    summed = lax.psum_scatter(
        head_partial.astype(jnp.bfloat16), "tensor", scatter_dimension=1, tiled=True
    ).astype(jnp.float32)
    mixed_rows = jnp.where(is_live[:, None], placed.astype(jnp.float32) + summed, 0.0).astype(
        jnp.bfloat16
    )
    key_value = jnp.stack(
        [keys_rot.reshape(row_count, head_width), values_all.reshape(row_count, head_width)], axis=1
    )
    pool_ids = jnp.arange(cache_pool.shape[0], dtype=jnp.int32)
    live_slot = jnp.where(is_live, cache_slot, -1)
    pool_source, pool_found = source_of(pool_ids, live_slot)
    new_pool = jnp.where(
        pool_found[:, None, None], jnp.take(key_value, pool_source, axis=0), cache_pool
    )
    return (mixed_rows, new_pool)


def solution(mesh):
    in_specs = (
        P("req", "tensor"),
        P("req"),
        P("req"),
        P("req"),
        P(),
        P(),
        P(None, None, "tensor"),
        P("tensor", None),
        P("req", None, "tensor"),
    )
    out_specs = (P("req", "tensor"), P("req", None, "tensor"))
    return jax.shard_map(shards, mesh=mesh, in_specs=in_specs, out_specs=out_specs, check_vma=False)
```

profile of v0, /device:TPU:1, one launch (start us, length us, event | category | flops | bytes accessed | tf_op | source)
XLA Modules:
  0.0 347.6 jit_solution(13693267671818737325)
XLA Ops:
  7.2 0.7 all-gather.2.cloned.1.call-update
  7.9 0.7 fusion.36
  8.6 0.6 fusion.28
  9.2 0.7 fusion.37
  9.9 0.5 select_reduce_fusion.2
  10.4 4.5 %gather_fusion = s32[1024]{0:T(1024)S(1)} fusion(s32[1024]{0:T(1024)S(1)} %get-tuple-element.15, s32[1024]{0:T(1024)S(1)} %broadcast_clamp_fusion.1), kind=kCustom, calls=%fused_computation.4 | custom fusion | bytes 12288 | tf_op jit(solution)/shard_map/gather | solution.py:99
  15.0 0.6 fusion.18
  15.6 0.7 select_n.139
  16.2 13.0 %all-to-all-start = ((s32[64,1,16]{2,1,0:T(1,128)}), s32[64,1,16]{2,1,0:T(1,128)S(1)}, u32[]{:S(2)}, u32[]{:S(2)}) async-start(s32[64,1,16]{2,1,0:T(1,128)} %bitcast.2), calls=%async_computation | async-start | bytes 65536 | tf_op jit(solution)/shard_map/all_to_all | solution.py:120
  29.3 8.8 %copy.52 = bf16[2048,3,512]{0,2,1:T(8,128)(2,1)} copy(bf16[2048,3,512]{2,0,1:T(8,128)(2,1)} %param.19) | data formatting | bytes 12582912 | tf_op args[6]
  38.2 26.3 %all-gather.2.cloned.1.call-done = bf16[1024,2048]{1,0:T(8,128)(2,1)} async-done(((bf16[1024,512]{1,0:T(8,128)(2,1)}), bf16[1024,2048]{1,0:T(8,128)(2,1)}) %all-gather.2.cloned.1.call-update) | async-done | bytes 4194320 | tf_op jit(solution)/shard_map/all_gather | solution.py:47
  64.5 3.0 convert_reduce_fusion
  67.4 0.5 copy-done.2
  67.9 1.2 fusion.3
  69.2 11.1 %fusion.23 = bf16[1024,1536]{1,0:T(8,128)(2,1)} fusion(bf16[2048,1536]{0,1:T(8,128)(2,1)} %bitcast.36, bf16[1024,2048]{1,0:T(8,128)(2,1)S(1)} %copy-done.2, f32[2048]{0:T(1024)S(1)} %convert_element_type.87, f32[2048]{0:T(1024)S(1)} %convert_element_type.86, f32[1024]{0:T(1024)S(1)} %add_rsqrt_fusion, f32[1024]{0:T(1024)S(1)} %broadcast_multiply_fusion), kind=kOutput, calls=%fused_computation.44 | convolution fusion | flops 6456606720 | bytes 13656064 | tf_op jit(solution)/shard_map/dot_general | solution.py:50
  80.3 9.6 %gather_fusion.4 = bf16[1024,1536]{1,0:T(8,128)(2,1)} fusion(bf16[1024,1536]{1,0:T(8,128)(2,1)} %fusion.23, s32[1024]{0:T(1024)S(1)} %fusion.39), kind=kCustom, calls=%fused_computation.1.clone | custom fusion | bytes 6295552 | tf_op jit(solution)/shard_map/jit(_take)/gather | solution.py:103
  89.9 3.5 %select_select_fusion.1 = bf16[1024,1536]{1,0:T(8,128)(2,1)} fusion(bf16[1024,1536]{1,0:T(8,128)(2,1)} %gather_fusion.4, pred[1024]{0:T(1024)(128)(4,1)S(1)} %compare_and_fusion.2, pred[1024]{0:T(1024)(128)(4,1)S(1)} %fusion.18), kind=kLoop, calls=%fused_computation.47 | loop fusion | flops 3145728 | bytes 6293504 | tf_op jit(solution)/shard_map/jit(_where)/select_n | solution.py:102
  93.4 11.0 %all-to-all-start.2 = ((bf16[64,16,1536]{2,1,0:T(8,128)(2,1)}), bf16[64,16,1536]{2,1,0:T(8,128)(2,1)}, u32[]{:S(2)}, u32[]{:S(2)}) async-start(bf16[64,16,1536]{2,1,0:T(8,128)(2,1)} %bitcast.35), calls=%async_computation.2 | async-start | bytes 6291456 | tf_op jit(solution)/shard_map/all_to_all | solution.py:119
  104.4 0.2 reduce-scatter.2.cloned.1.call-start
  104.6 0.4 convert_reduce_fusion.1
  105.0 0.5 multiply_cosine_fusion
  105.6 1.6 fusion.20
  107.1 0.5 broadcast.251
  107.7 0.7 reduce.3
  108.5 0.6 fusion.17
  109.0 0.5 select_reduce_fusion.1
  109.6 68.2 %all-to-all-done.2 = bf16[64,16,1536]{2,1,0:T(8,128)(2,1)} async-done(((bf16[64,16,1536]{2,1,0:T(8,128)(2,1)}), bf16[64,16,1536]{2,1,0:T(8,128)(2,1)}, u32[]{:S(2)}, u32[]{:S(2)}) %all-to-all-start.2) | async-done | bytes 3145760 | tf_op jit(solution)/shard_map/all_to_all | solution.py:119
  177.8 9.6 %gather_fusion.5 = bf16[1024,1536]{1,0:T(8,128)(2,1)} fusion(bf16[1024,1536]{1,0:T(8,128)(2,1)} %bitcast.7, s32[1024]{0:T(1024)S(1)} %fusion.40), kind=kCustom, calls=%fused_computation.3.clone | custom fusion | bytes 6295552 | tf_op jit(solution)/shard_map/jit(_take)/gather | solution.py:112
  187.3 3.5 %select_select_fusion = bf16[1024,1536]{1,0:T(8,128)(2,1)} fusion(bf16[1024,1536]{1,0:T(8,128)(2,1)} %gather_fusion.5, pred[1024]{0:T(1024)(128)(4,1)S(1)} %compare_and_fusion.1, pred[1024]{0:T(1024)(128)(4,1)S(1)} %fusion.17), kind=kLoop, calls=%fused_computation.46 | loop fusion | flops 3145728 | bytes 6293504 | tf_op jit(solution)/shard_map/jit(_where)/select_n | solution.py:110
  190.8 4.7 %copy.53 = bf16[1024,1536]{0,1:T(8,128)(2,1)} copy(bf16[1024,1536]{1,0:T(8,128)(2,1)} %select_select_fusion) | data formatting | bytes 6291456 | tf_op jit(solution)/shard_map/jit(_where)/select_n | solution.py:110
  195.5 3.6 %fusion.46 = (bf16[1024,1,2,256]{0,3,2,1:T(8,128)(2,1)}, bf16[1024,1,2,256]{0,3,2,1:T(8,128)(2,1)}, bf16[1024,2,256]{0,2,1:T(8,128)(2,1)}) fusion(bf16[1024,3,2,256]{0,3,2,1:T(8,128)(2,1)} %bitcast.33), kind=kLoop, calls=%fused_computation.111 | loop fusion | bytes 6291456 | tf_op jit(solution)/shard_map/slice | solution.py:132
  199.1 1.5 copy.66
  200.8 0.4 slice.63
  201.2 1.0 slice.60
  202.2 0.9 slice.68
  203.2 0.8 slice_convert_fusion
  204.0 2.4 copy.57
  206.4 1.3 multiply_subtract_fusion
  207.7 1.1 pad_maximum_fusion.1
  208.8 2.0 copy.58
  210.8 1.5 copy.54
  212.3 0.3 subtract_convert_fusion
  212.6 0.3 pad_maximum_fusion.2
  213.0 1.5 maximum_convert_fusion
  214.5 1.0 copy-done.3
  215.6 1.3 fusion.29
  216.9 8.0 %fusion.47 = (f32[2,1024]{1,0:T(2,128)S(1)}, f32[2,1024,1024]{1,2,0:T(8,128)}) fusion(f32[2,1024,1024]{1,2,0:T(8,128)S(1)} %fusion.29, pred[1024,1024]{0,1:T(8,128)(4,1)} %fusion.20), kind=kOutput, calls=%fused_computation.112 | output fusion | flops 14681087 | bytes 17833984 | tf_op jit(solution)/shard_map/sub | solution.py:56
  224.8 5.0 %fusion.26 = bf16[2,256,1024]{2,1,0:T(8,128)(2,1)S(1)} fusion(f32[2,1024,1024]{1,2,0:T(8,128)} %get-tuple-element.18, f32[2,1024]{1,0:T(2,128)S(1)} %compare_select_fusion.1, bf16[1024,3,2,256]{0,3,2,1:T(8,128)(2,1)} %bitcast.34), kind=kOutput, calls=%fused_computation.51 | convolution fusion | flops 1078460416 | bytes 10493952 | tf_op jit(solution)/shard_map/hqk,khd->qhd/dot_general | solution.py:138
  229.8 4.3 %convolution_convert_fusion = bf16[1024,2048]{1,0:T(8,128)(2,1)} fusion(bf16[1024,512]{0,1:T(8,128)(2,1)S(1)} %bitcast.48, bf16[512,2048]{1,0:T(8,128)(2,1)S(1)} %copy-done), kind=kOutput, calls=%fused_computation.45 | convolution fusion | flops 2149580800 | bytes 7340032 | tf_op jit(solution)/shard_map/dot_general | solution.py:140
  234.2 1.2 copy-done.1
  235.4 5.1 %gather_fusion.2 = bf16[1024,512]{1,0:T(8,128)(2,1)} fusion(bf16[1024,512]{1,0:T(8,128)(2,1)S(1)} %copy-done.1, s32[1024]{0:T(1024)S(1)} %fusion.39), kind=kCustom, calls=%fused_computation.clone | custom fusion | bytes 2101248 | tf_op jit(solution)/shard_map/jit(_take)/gather | solution.py:103
  240.4 2.7 select_select_fusion.3
  243.1 6.0 %all-to-all-start.1 = ((bf16[64,16,512]{2,1,0:T(8,128)(2,1)}), bf16[64,16,512]{2,1,0:T(8,128)(2,1)S(1)}, u32[]{:S(2)}, u32[]{:S(2)}) async-start(bf16[64,16,512]{2,1,0:T(8,128)(2,1)} %bitcast.38), calls=%async_computation.1 | async-start | bytes 2097152 | tf_op jit(solution)/shard_map/all_to_all | solution.py:118
  249.2 1.0 fusion.7
  250.2 0.9 select_reduce_fusion
  251.2 26.5 %all-to-all-done.1 = bf16[64,16,512]{2,1,0:T(8,128)(2,1)S(1)} async-done(((bf16[64,16,512]{2,1,0:T(8,128)(2,1)}), bf16[64,16,512]{2,1,0:T(8,128)(2,1)S(1)}, u32[]{:S(2)}, u32[]{:S(2)}) %all-to-all-start.1) | async-done | bytes 1048608 | tf_op jit(solution)/shard_map/all_to_all | solution.py:118
  277.7 5.1 %gather_fusion.3 = bf16[1024,512]{1,0:T(8,128)(2,1)} fusion(bf16[1024,512]{1,0:T(8,128)(2,1)S(1)} %bitcast.32, s32[1024]{0:T(1024)S(1)} %fusion.40), kind=kCustom, calls=%fused_computation.2.clone | custom fusion | bytes 2101248 | tf_op jit(solution)/shard_map/jit(_take)/gather | solution.py:112
  282.8 1.5 copy.61
  284.3 6.0 %copy.63 = bf16[1024,1,512]{2,1,0:T(2,128)(2,1)} copy(bf16[1024,1,512]{0,2,1:T(8,128)(2,1)} %bitcast.39) | data formatting | bytes 2097152 | tf_op jit(solution)/shard_map/stack;reshape;squeeze | solution.py:149
  290.2 3.9 %copy.62 = bf16[1024,1,512]{2,1,0:T(2,128)(2,1)} copy(bf16[1024,1,512]{0,2,1:T(8,128)(2,1)S(1)} %bitcast.37) | data formatting | bytes 2097152 | tf_op jit(solution)/shard_map/convert_element_type | solution.py:43
  294.2 6.7 %pad_maximum_fusion = bf16[1024,2,512]{2,1,0:T(2,128)(2,1)} fusion(bf16[1024,1,512]{2,1,0:T(2,128)(2,1)} %copy.63, bf16[1024,1,512]{2,1,0:T(2,128)(2,1)} %copy.62), kind=kLoop, calls=%fused_computation.49 | loop fusion | flops 4194304 | bytes 4194304 | tf_op jit(solution)/shard_map/stack | solution.py:149
  300.9 22.9 %gather_fusion.1 = bf16[2048,2,512]{2,1,0:T(2,128)(2,1)} fusion(bf16[1024,2,512]{2,1,0:T(2,128)(2,1)} %pad_maximum_fusion, s32[2048]{0:T(1024)S(1)} %broadcast_clamp_fusion), kind=kCustom, calls=%fused_computation.5 | custom fusion | bytes 8396800 | tf_op jit(solution)/shard_map/jit(_take)/gather | solution.py:156
  323.8 14.1 %broadcast_select_fusion = bf16[2048,2,512]{2,1,0:T(2,128)(2,1)} fusion(bf16[2048,2,512]{2,1,0:T(2,128)(2,1)} %param.21, pred[2048]{0:T(1024)(128)(4,1)S(1)} %fusion.7, bf16[2048,2,512]{2,1,0:T(2,128)(2,1)} %gather_fusion.1, pred[2048]{0:T(1024)(128)(4,1)S(1)} %compare_and_fusion), kind=kLoop, calls=%fused_computation.21 | loop fusion | flops 4194304 | bytes 12587008 | tf_op jit(solution)/shard_map/jit(_where)/select_n | solution.py:155
  337.9 2.8 select_convert_fusion
  (44 shorter events, 0.5 us)
Async XLA Ops:
  7.2 222.7 %copy-start = (bf16[512,2048]{1,0:T(8,128)(2,1)S(1)}, bf16[512,2048]{1,0:T(8,128)(2,1)}, u32[]{:S(2)}) copy-start(bf16[512,2048]{1,0:T(8,128)(2,1)} %param.20) | copy-start | bytes 6291460
  7.2 57.3 %all-gather.2.cloned.1.call-start = ((), (), s32[]{:S(2)}) async-start(), calls=%async_computation.4 | async-start | bytes 5242880 | tf_op jit(solution)/shard_map/all_gather | solution.py:47
  16.2 77.1 %all-to-all-start = ((s32[64,1,16]{2,1,0:T(1,128)}), s32[64,1,16]{2,1,0:T(1,128)S(1)}, u32[]{:S(2)}, u32[]{:S(2)}) async-start(s32[64,1,16]{2,1,0:T(1,128)} %bitcast.2), calls=%async_computation | async-start | bytes 65536 | tf_op jit(solution)/shard_map/all_to_all | solution.py:120
  29.2 8.9 %copy-start.8 = (bf16[2048]{0:T(1024)(128)(2,1)S(1)}, bf16[2048]{0:T(1024)(128)(2,1)}, u32[]{:S(2)}) copy-start(bf16[2048]{0:T(1024)(128)(2,1)} %param.18) | copy-start | bytes 12292
  29.3 8.9 %copy-start.9 = (bf16[2048]{0:T(1024)(128)(2,1)S(1)}, bf16[2048]{0:T(1024)(128)(2,1)}, u32[]{:S(2)}) copy-start(bf16[2048]{0:T(1024)(128)(2,1)} %param.17) | copy-start | bytes 12292
  64.5 3.4 copy-start.2
  93.3 11.3 %copy-start.7 = (s32[1024]{0:T(1024)S(1)}, s32[1024]{0:T(1024)}, u32[]{:S(2)}) copy-start(s32[1024]{0:T(1024)} %param.15) | copy-start | bytes 12292
  93.4 84.4 %all-to-all-start.2 = ((bf16[64,16,1536]{2,1,0:T(8,128)(2,1)}), bf16[64,16,1536]{2,1,0:T(8,128)(2,1)}, u32[]{:S(2)}, u32[]{:S(2)}) async-start(bf16[64,16,1536]{2,1,0:T(8,128)(2,1)} %bitcast.35), calls=%async_computation.2 | async-start | bytes 6291456 | tf_op jit(solution)/shard_map/all_to_all | solution.py:119
  104.4 233.6 %reduce-scatter.2.cloned.1.call-start = ((), (), s32[]{:S(2)}) async-start(), calls=%async_computation.5 | async-start | bytes 5242880 | tf_op jit(solution)/shard_map/reduce_scatter | solution.py:143
  200.6 1.6 copy-start.5
  210.8 4.8 %copy-start.6 = (bf16[1024,2,192]{0,2,1:T(8,128)(2,1)S(1)}, bf16[1024,2,192]{0,2,1:T(8,128)(2,1)}, u32[]{:S(2)}) copy-start(bf16[1024,2,192]{0,2,1:T(8,128)(2,1)} %slice.68) | copy-start | bytes 2359300
  214.5 1.1 copy-start.3
  234.1 1.2 copy-start.1
  240.4 8.7 %copy-start.10 = (s32[1024]{0:T(1024)S(1)}, s32[1024]{0:T(1024)}, u32[]{:S(2)}) copy-start(s32[1024]{0:T(1024)} %param.16) | copy-start | bytes 12292
  243.1 34.6 %all-to-all-start.1 = ((bf16[64,16,512]{2,1,0:T(8,128)(2,1)}), bf16[64,16,512]{2,1,0:T(8,128)(2,1)S(1)}, u32[]{:S(2)}, u32[]{:S(2)}) async-start(bf16[64,16,512]{2,1,0:T(8,128)(2,1)} %bitcast.38), calls=%async_computation.1 | async-start | bytes 2097152 | tf_op jit(solution)/shard_map/all_to_all | solution.py:118
  323.8 14.1 %copy-start.4 = (bf16[1024,512]{1,0:T(8,128)(2,1)S(1)}, bf16[1024,512]{1,0:T(8,128)(2,1)}, u32[]{:S(2)}) copy-start(bf16[1024,512]{1,0:T(8,128)(2,1)} %gather_fusion.3) | copy-start | bytes 3145732
Sparse Core Ops, SparseCore 0:
  9.8 54.5 all-gather.1
  234.3 45.1 reduce-scatter.1
where the time goes:
time: 349 us; the launch traced here: 348 us
  waiting for transfers between devices  122 us (35%)
  local copies, waits for them, and re-layouts  99.1 us (28%)
  other arithmetic  59.8 us (17%)
  starting transfers between devices  30.3 us (9%)
  matrix products  22.3 us (6%)
  between operations  14.4 us (4%)
    all_to_all x1, waiting for transfers between devices, shards(): lax.all_to_all(pack(projected), 'req', split_axis=0, concat_axis=0, tiled...  68.2 us
    all_to_all x1, waiting for transfers between devices, shards(): lax.all_to_all(pack(stream), 'req', split_axis=0, concat_axis=0, tiled=True)  26.5 us
    all_gather x1, waiting for transfers between devices, project(): features_all = lax.all_gather(split_rows, 'tensor', axis=1, tiled=True)  26.3 us
    gather x1, local copies, waits for them, and re-layouts, shards(): jnp.take(key_value, pool_source, axis=0)  22.9 us
    gather x2, local copies, waits for them, and re-layouts, pack(): jnp.take(values, send_source, axis=0)  14.6 us
    gather x2, local copies, waits for them, and re-layouts, unpack(): jnp.take(flat_values, arrived_source, axis=0)  14.6 us
    select_n x1, other arithmetic, shards(): jnp.where(pool_found[:, None, None], jnp.take(key_value, pool_source, axi...  14.1 us
    unnamed x24, local copies, waits for them, and re-layouts  13.1 us
  transfers between devices with their start and end apart: 5, of which 3 were waited for; matrix products, arithmetic and copies ran while one was open for 35% of the time, Pallas kernels for 0%

commit v1 on v0

--- a/solution.py
+++ b/solution.py
@@ -44,7 +44,18 @@
 
 
 def project(split_rows, norm_gain, norm_bias, projection):
-    features_all = lax.all_gather(split_rows, "tensor", axis=1, tiled=True)
+    ways = lax.axis_size("tensor")
+    up = [(d, (d + 1) % ways) for d in range(ways)]
+    down = [(d, (d - 1) % ways) for d in range(ways)]
+    earlier, later = ([split_rows], [split_rows])
+    for _ in range(ways // 2):
+        earlier.append(lax.ppermute(earlier[-1], "tensor", up))
+    for _ in range((ways - 1) // 2):
+        later.append(lax.ppermute(later[-1], "tensor", down))
+    line = jnp.concatenate([*earlier[::-1], *later[1:]], axis=1)
+    features_all = jnp.roll(
+        line, (lax.axis_index("tensor") - ways // 2) * split_rows.shape[1], axis=1
+    )
     normed = layer_norm(features_all, norm_gain, norm_bias)
     flat_weight = projection.reshape(projection.shape[0], projection.shape[1] * projection.shape[2])
     return jnp.dot(normed, flat_weight, preferred_element_type=jnp.float32).astype(jnp.bfloat16)

time: 349 us -> 366 us (1.049); the launches traced: 348 us -> 360 us
  waiting for transfers between devices: 122 us -> 101 us
  starting transfers between devices: 30.3 us -> 48 us
  local copies, waits for them, and re-layouts: 99.1 us -> 108 us
  other arithmetic: 59.8 us -> 64.7 us
    all_gather x1 -> x0, waiting for transfers between devices: 26.3 us -> none  [project(): features_all = lax.all_gather(split_rows, 'tensor', axis=1, tiled=True)]
    ppermute x0 -> x3, waiting for transfers between devices: none -> 18.6 us  [the longest x2 18.6 us: project(): earlier.append(lax.ppermute(earlier[-1], 'tensor', up))]
    all_to_all x1, waiting for transfers between devices: 68.2 us -> 56.3 us  [shards(): lax.all_to_all(pack(projected), 'req', split_axis=0, concat_axis=0, tiled...]
    reduce_scatter x1, starting transfers between devices: 0.22 us -> 12 us  [shards(): lax.psum_scatter(head_partial.astype(jnp.bfloat16), 'tensor', scatter_dim...]
    unnamed x24 -> x35, local copies, waits for them, and re-layouts: 13.1 us -> 19.2 us
    sub x1, other arithmetic: 7.96 us -> 13.5 us  [masked_softmax(): raised = jnp.where(allowed[None], jnp.exp(scores - top_score), 0.0)]
    ppermute x0 -> x3, starting transfers between devices: none -> 5.28 us  [the longest x2 3.75 us: project(): earlier.append(lax.ppermute(earlier[-1], 'tensor', up))]
  transfers between devices with their start and end apart: 5 -> 7, of which waited for: 3 -> 3; matrix products, arithmetic and copies ran while one was open for 35% -> 35% of each run, Pallas kernels for 0% -> 0%
where the time goes in v1:
time: 366 us; the launch traced here: 360 us
  local copies, waits for them, and re-layouts  108 us (30%)
  waiting for transfers between devices  101 us (28%)
  other arithmetic  64.7 us (18%)
  starting transfers between devices  48 us (13%)
  matrix products  23.7 us (6%)
  between operations  14.7 us (4%)
    all_to_all x1, waiting for transfers between devices, shards(): lax.all_to_all(pack(projected), 'req', split_axis=0, concat_axis=0, tiled...  56.3 us
    all_to_all x1, waiting for transfers between devices, shards(): lax.all_to_all(pack(stream), 'req', split_axis=0, concat_axis=0, tiled=True)  26.5 us
    gather x1, local copies, waits for them, and re-layouts, shards(): jnp.take(key_value, pool_source, axis=0)  22.9 us
    unnamed x35, local copies, waits for them, and re-layouts  19.2 us
    ppermute x2, waiting for transfers between devices, project(): earlier.append(lax.ppermute(earlier[-1], 'tensor', up))  18.6 us
    gather x2, local copies, waits for them, and re-layouts, pack(): jnp.take(values, send_source, axis=0)  14.7 us
    gather x2, local copies, waits for them, and re-layouts, unpack(): jnp.take(flat_values, arrived_source, axis=0)  14.6 us
    select_n x1, other arithmetic, shards(): jnp.where(pool_found[:, None, None], jnp.take(key_value, pool_source, axi...  14.1 us
  transfers between devices with their start and end apart: 7, of which 3 were waited for; matrix products, arithmetic and copies ran while one was open for 35% of the time, Pallas kernels for 0%

profile of v1, /device:TPU:1, one launch (start us, length us, event | category | flops | bytes accessed | tf_op | source)
XLA Modules:
  0.0 360.2 jit_solution(2202682108734637085)
XLA Ops:
  7.2 2.2 collective-permute-start
  9.4 1.5 collective-permute-start.2
  10.9 0.7 fusion.37
  11.6 0.6 fusion.29
  12.2 0.7 fusion.38
  13.4 18.5 %collective-permute-done = bf16[1024,512]{1,0:T(8,128)(2,1)} collective-permute-done((bf16[1024,512]{1,0:T(8,128)(2,1)}, bf16[1024,512]{1,0:T(8,128)(2,1)}, u32[]{:S(2)}, u32[]{:S(2)}) %collective-permute-start) | collective-permute-done | bytes 1048608 | tf_op jit(solution)/shard_map/ppermute | solution.py:52
  32.0 1.5 collective-permute-start.1
  33.5 4.5 %gather_fusion = s32[1024]{0:T(1024)S(1)} fusion(s32[1024]{0:T(1024)S(1)} %get-tuple-element.15, s32[1024]{0:T(1024)S(1)} %broadcast_clamp_fusion.1), kind=kCustom, calls=%fused_computation.4 | custom fusion | bytes 12288 | tf_op jit(solution)/shard_map/gather | solution.py:110
  38.1 0.6 fusion.18
  38.6 0.7 select_n.151
  39.3 14.0 %all-to-all-start = ((s32[64,1,16]{2,1,0:T(1,128)}), s32[64,1,16]{2,1,0:T(1,128)S(1)}, u32[]{:S(2)}, u32[]{:S(2)}) async-start(s32[64,1,16]{2,1,0:T(1,128)} %bitcast.2), calls=%async_computation | async-start | bytes 65536 | tf_op jit(solution)/shard_map/all_to_all | solution.py:131
  53.4 8.8 %copy.52 = bf16[2048,3,512]{0,2,1:T(8,128)(2,1)} copy(bf16[2048,3,512]{2,0,1:T(8,128)(2,1)} %param.19) | data formatting | bytes 12582912 | tf_op args[6]
  62.3 1.4 constant_dynamic-update-slice_fusion.7
  63.7 1.3 constant_dynamic-update-slice_fusion.6
  65.2 1.3 constant_dynamic-update-slice_fusion.4
  66.6 1.3 constant_dynamic-update-slice_fusion.3
  67.9 1.3 constant_dynamic-update-slice_fusion.2
  69.4 1.5 constant_dynamic-update-slice_fusion
  70.9 0.6 convert_reduce_fusion
  71.6 1.2 fusion.3
  72.9 9.2 %fusion.23 = bf16[1024,1536]{1,0:T(8,128)(2,1)} fusion(bf16[2048,1536]{0,1:T(8,128)(2,1)S(1)} %bitcast.38, f32[2048]{0:T(1024)S(1)} %convert_element_type.87, f32[2048]{0:T(1024)S(1)} %convert_element_type.86, f32[1024]{0:T(1024)S(1)} %add_rsqrt_fusion, f32[1024]{0:T(1024)S(1)} %broadcast_multiply_fusion, ...), kind=kOutput, calls=%fused_computation.44 | convolution fusion | flops 6456606720 | bytes 13656068 | tf_op jit(solution)/shard_map/dot_general | solution.py:61
  82.0 9.6 %gather_fusion.4 = bf16[1024,1536]{1,0:T(8,128)(2,1)} fusion(bf16[1024,1536]{1,0:T(8,128)(2,1)} %fusion.23, s32[1024]{0:T(1024)S(1)} %fusion.40), kind=kCustom, calls=%fused_computation.1.clone | custom fusion | bytes 6295552 | tf_op jit(solution)/shard_map/jit(_take)/gather | solution.py:114
  91.6 3.5 select_select_fusion.1
  95.1 10.6 %all-to-all-start.2 = ((bf16[64,16,1536]{2,1,0:T(8,128)(2,1)}), bf16[64,16,1536]{2,1,0:T(8,128)(2,1)}, u32[]{:S(2)}, u32[]{:S(2)}) async-start(bf16[64,16,1536]{2,1,0:T(8,128)(2,1)} %bitcast.35), calls=%async_computation.2 | async-start | bytes 6291456 | tf_op jit(solution)/shard_map/all_to_all | solution.py:130
  105.7 12.0 %reduce-scatter.2.cloned.1.call-start = ((), (), s32[]{:S(2)}) async-start(), calls=%async_computation.4 | async-start | bytes 5242880 | tf_op jit(solution)/shard_map/reduce_scatter | solution.py:154
  118.7 1.7 fusion.20
  120.9 0.7 reduce.3
  121.7 0.6 fusion.17
  122.8 56.3 %all-to-all-done.2 = bf16[64,16,1536]{2,1,0:T(8,128)(2,1)} async-done(((bf16[64,16,1536]{2,1,0:T(8,128)(2,1)}), bf16[64,16,1536]{2,1,0:T(8,128)(2,1)}, u32[]{:S(2)}, u32[]{:S(2)}) %all-to-all-start.2) | async-done | bytes 3145760 | tf_op jit(solution)/shard_map/all_to_all | solution.py:130
  179.2 9.6 %gather_fusion.5 = bf16[1024,1536]{1,0:T(8,128)(2,1)} fusion(bf16[1024,1536]{1,0:T(8,128)(2,1)} %bitcast.7, s32[1024]{0:T(1024)S(1)} %fusion.41), kind=kCustom, calls=%fused_computation.3.clone | custom fusion | bytes 6295552 | tf_op jit(solution)/shard_map/jit(_take)/gather | solution.py:123
  188.7 3.5 select_select_fusion
  192.2 4.6 %copy.53 = bf16[1024,1536]{0,1:T(8,128)(2,1)} copy(bf16[1024,1536]{1,0:T(8,128)(2,1)} %select_select_fusion) | data formatting | bytes 6291456 | tf_op jit(solution)/shard_map/jit(_where)/select_n | solution.py:121
  196.9 3.6 fusion.48
  200.5 2.3 copy.66
  202.7 1.5 bitcast_convert_fusion
  204.2 1.0 slice.60
  205.2 1.3 slice.63
  206.6 0.8 slice_convert_fusion
  207.4 0.9 slice.68
  208.4 2.4 copy.57
  210.7 1.3 multiply_subtract_fusion
  212.1 1.1 pad_maximum_fusion.1
  213.1 2.0 copy.58
  215.1 1.5 copy.54
  217.3 1.9 maximum_convert_fusion
  219.2 1.0 copy-done.2
  220.2 4.5 %fusion.30 = f32[2,1024,1024]{1,2,0:T(8,128)} fusion(bf16[1024,2,256]{2,0,1:T(8,128)(2,1)S(1)} %maximum_convert_fusion, bf16[1024,2,192]{0,2,1:T(8,128)(2,1)S(1)} %copy-done.5, bf16[1024,2,64]{0,2,1:T(8,128)(2,1)S(1)} %copy.55), kind=kOutput, calls=%fused_computation.56 | convolution fusion | flops 1075838976 | bytes 10485760 | tf_op jit(solution)/shard_map/qhd,khd->hqk/dot_general | solution.py:145
  224.7 13.5 %fusion.49 = (f32[2,1024]{1,0:T(2,128)S(1)}, f32[2,1024,1024]{1,2,0:T(8,128)}) fusion(f32[2,1024,1024]{1,2,0:T(8,128)} %fusion.30, pred[1024,1024]{0,1:T(8,128)(4,1)S(1)} %copy-done.6), kind=kOutput, calls=%fused_computation.122 | output fusion | flops 14681087 | bytes 17833984 | tf_op jit(solution)/shard_map/sub | solution.py:67
  238.2 5.0 %fusion.27 = bf16[2,256,1024]{2,1,0:T(8,128)(2,1)S(1)} fusion(f32[2,1024,1024]{1,2,0:T(8,128)} %get-tuple-element.18, f32[2,1024]{1,0:T(2,128)S(1)} %compare_select_fusion.1, bf16[1024,3,2,256]{0,3,2,1:T(8,128)(2,1)} %bitcast.34), kind=kOutput, calls=%fused_computation.52 | convolution fusion | flops 1078460416 | bytes 10493952 | tf_op jit(solution)/shard_map/hqk,khd->qhd/dot_general | solution.py:149
  243.2 4.5 %convolution_convert_fusion = bf16[1024,2048]{1,0:T(8,128)(2,1)} fusion(bf16[1024,512]{0,1:T(8,128)(2,1)S(1)} %bitcast.50, bf16[512,2048]{1,0:T(8,128)(2,1)S(1)} %copy-done), kind=kOutput, calls=%fused_computation.45 | convolution fusion | flops 2149580800 | bytes 7340032 | tf_op jit(solution)/shard_map/dot_general | solution.py:151
  247.7 5.1 %gather_fusion.2 = bf16[1024,512]{1,0:T(8,128)(2,1)} fusion(bf16[1024,512]{1,0:T(8,128)(2,1)S(1)} %copy-done.1, s32[1024]{0:T(1024)S(1)} %fusion.40), kind=kCustom, calls=%fused_computation.clone | custom fusion | bytes 2101248 | tf_op jit(solution)/shard_map/jit(_take)/gather | solution.py:114
  252.8 2.6 select_select_fusion.3
  255.4 6.1 %all-to-all-start.1 = ((bf16[64,16,512]{2,1,0:T(8,128)(2,1)}), bf16[64,16,512]{2,1,0:T(8,128)(2,1)S(1)}, u32[]{:S(2)}, u32[]{:S(2)}) async-start(bf16[64,16,512]{2,1,0:T(8,128)(2,1)} %bitcast.40), calls=%async_computation.1 | async-start | bytes 2097152 | tf_op jit(solution)/shard_map/all_to_all | solution.py:129
  261.5 1.0 fusion.7
  262.6 0.9 select_reduce_fusion
  263.6 26.5 %all-to-all-done.1 = bf16[64,16,512]{2,1,0:T(8,128)(2,1)S(1)} async-done(((bf16[64,16,512]{2,1,0:T(8,128)(2,1)}), bf16[64,16,512]{2,1,0:T(8,128)(2,1)S(1)}, u32[]{:S(2)}, u32[]{:S(2)}) %all-to-all-start.1) | async-done | bytes 1048608 | tf_op jit(solution)/shard_map/all_to_all | solution.py:129
  290.1 5.1 %gather_fusion.3 = bf16[1024,512]{1,0:T(8,128)(2,1)} fusion(bf16[1024,512]{1,0:T(8,128)(2,1)S(1)} %bitcast.32, s32[1024]{0:T(1024)S(1)} %fusion.41), kind=kCustom, calls=%fused_computation.2.clone | custom fusion | bytes 2101248 | tf_op jit(solution)/shard_map/jit(_take)/gather | solution.py:123
  295.1 1.5 copy.61
  296.6 3.9 %copy.62 = bf16[1024,1,512]{2,1,0:T(2,128)(2,1)} copy(bf16[1024,1,512]{0,2,1:T(8,128)(2,1)S(1)} %bitcast.39) | data formatting | bytes 2097152 | tf_op jit(solution)/shard_map/convert_element_type | solution.py:43
  300.6 6.0 %copy.63 = bf16[1024,1,512]{2,1,0:T(2,128)(2,1)} copy(bf16[1024,1,512]{0,2,1:T(8,128)(2,1)} %bitcast.41) | data formatting | bytes 2097152 | tf_op jit(solution)/shard_map/stack;reshape;squeeze | solution.py:160
  306.5 6.7 %pad_maximum_fusion = bf16[1024,2,512]{2,1,0:T(2,128)(2,1)} fusion(bf16[1024,1,512]{2,1,0:T(2,128)(2,1)} %copy.63, bf16[1024,1,512]{2,1,0:T(2,128)(2,1)} %copy.62), kind=kLoop, calls=%fused_computation.50 | loop fusion | flops 4194304 | bytes 4194304 | tf_op jit(solution)/shard_map/stack | solution.py:160
  313.3 22.9 %gather_fusion.1 = bf16[2048,2,512]{2,1,0:T(2,128)(2,1)} fusion(bf16[1024,2,512]{2,1,0:T(2,128)(2,1)} %pad_maximum_fusion, s32[2048]{0:T(1024)S(1)} %broadcast_clamp_fusion), kind=kCustom, calls=%fused_computation.5 | custom fusion | bytes 8396800 | tf_op jit(solution)/shard_map/jit(_take)/gather | solution.py:167
  336.2 14.1 %broadcast_select_fusion = bf16[2048,2,512]{2,1,0:T(2,128)(2,1)} fusion(bf16[2048,2,512]{2,1,0:T(2,128)(2,1)} %param.21, pred[2048]{0:T(1024)(128)(4,1)S(1)} %fusion.7, bf16[2048,2,512]{2,1,0:T(2,128)(2,1)} %gather_fusion.1, pred[2048]{0:T(1024)(128)(4,1)S(1)} %compare_and_fusion), kind=kLoop, calls=%fused_computation.21 | loop fusion | flops 4194304 | bytes 12587008 | tf_op jit(solution)/shard_map/jit(_where)/select_n | solution.py:166
  350.3 2.8 select_convert_fusion
  (60 shorter events, 3.7 us)
Async XLA Ops:
  7.2 236.0 %copy-start = (bf16[512,2048]{1,0:T(8,128)(2,1)S(1)}, bf16[512,2048]{1,0:T(8,128)(2,1)}, u32[]{:S(2)}) copy-start(bf16[512,2048]{1,0:T(8,128)(2,1)} %param.20) | copy-start | bytes 6291460
  7.2 24.8 %collective-permute-start = (bf16[1024,512]{1,0:T(8,128)(2,1)}, bf16[1024,512]{1,0:T(8,128)(2,1)}, u32[]{:S(2)}, u32[]{:S(2)}) collective-permute-start(bf16[1024,512]{1,0:T(8,128)(2,1)} %param.13), channel_id=1, source_target_pairs={{0,1},{1,2},{2,3},{3,0},{4,5},{5,6},{6,7},{7,4},{8,9},{9,10},{10,1... | collective-permute-start | bytes 3145736 | tf_op jit(solution)/shard_map/ppermute | solution.py:52
  9.4 55.8 %collective-permute-start.2 = (bf16[1024,512]{1,0:T(8,128)(2,1)}, bf16[1024,512]{1,0:T(8,128)(2,1)}, u32[]{:S(2)}, u32[]{:S(2)}) collective-permute-start(bf16[1024,512]{1,0:T(8,128)(2,1)} %param.13), channel_id=1, source_target_pairs={{0,3},{1,0},{2,1},{3,2},{4,7},{5,4},{6,5},{7,6},{8,11},{9,8},{10,9... | collective-permute-start | bytes 3145736 | tf_op jit(solution)/shard_map/ppermute | solution.py:54
  32.0 30.3 %collective-permute-start.1 = (bf16[1024,512]{1,0:T(8,128)(2,1)}, bf16[1024,512]{1,0:T(8,128)(2,1)}, u32[]{:S(2)}, u32[]{:S(2)}) collective-permute-start(bf16[1024,512]{1,0:T(8,128)(2,1)} %collective-permute-done), channel_id=1, source_target_pairs={{0,1},{1,2},{2,3},{3,0},{4,5},{5,6},{6,7},{7,4},{8,9},{9,10},{10,1... | collective-permute-start | bytes 3145736 | tf_op jit(solution)/shard_map/ppermute | solution.py:52
  39.3 55.8 %all-to-all-start = ((s32[64,1,16]{2,1,0:T(1,128)}), s32[64,1,16]{2,1,0:T(1,128)S(1)}, u32[]{:S(2)}, u32[]{:S(2)}) async-start(s32[64,1,16]{2,1,0:T(1,128)} %bitcast.2), calls=%async_computation | async-start | bytes 65536 | tf_op jit(solution)/shard_map/all_to_all | solution.py:131
  53.3 8.9 %copy-start.8 = (bf16[2048]{0:T(1024)(128)(2,1)S(1)}, bf16[2048]{0:T(1024)(128)(2,1)}, u32[]{:S(2)}) copy-start(bf16[2048]{0:T(1024)(128)(2,1)} %param.17) | copy-start | bytes 12292
  53.4 8.9 %copy-start.9 = (bf16[2048]{0:T(1024)(128)(2,1)S(1)}, bf16[2048]{0:T(1024)(128)(2,1)}, u32[]{:S(2)}) copy-start(bf16[2048]{0:T(1024)(128)(2,1)} %param.18) | copy-start | bytes 12292
  62.2 2.9 copy-start.1
  69.3 3.5 slice-start
  70.9 1.9 slice-start.1
  95.1 22.7 %copy-start.7 = (s32[1024]{0:T(1024)S(1)}, s32[1024]{0:T(1024)}, u32[]{:S(2)}) copy-start(s32[1024]{0:T(1024)} %param.15) | copy-start | bytes 12292
  95.1 84.1 %all-to-all-start.2 = ((bf16[64,16,1536]{2,1,0:T(8,128)(2,1)}), bf16[64,16,1536]{2,1,0:T(8,128)(2,1)}, u32[]{:S(2)}, u32[]{:S(2)}) async-start(bf16[64,16,1536]{2,1,0:T(8,128)(2,1)} %bitcast.35), calls=%async_computation.2 | async-start | bytes 6291456 | tf_op jit(solution)/shard_map/all_to_all | solution.py:130
  105.7 244.5 %reduce-scatter.2.cloned.1.call-start = ((), (), s32[]{:S(2)}) async-start(), calls=%async_computation.4 | async-start | bytes 5242880 | tf_op jit(solution)/shard_map/reduce_scatter | solution.py:154
  202.7 3.9 %copy-start.4 = (bf16[1024,2,256]{0,2,1:T(8,128)(2,1)S(1)}, bf16[1024,2,256]{0,2,1:T(8,128)(2,1)}, u32[]{:S(2)}) copy-start(bf16[1024,2,256]{0,2,1:T(8,128)(2,1)} %get-tuple-element.8) | copy-start | bytes 3145732
  215.1 5.1 %copy-start.5 = (bf16[1024,2,192]{0,2,1:T(8,128)(2,1)S(1)}, bf16[1024,2,192]{0,2,1:T(8,128)(2,1)}, u32[]{:S(2)}) copy-start(bf16[1024,2,192]{0,2,1:T(8,128)(2,1)} %slice.68) | copy-start | bytes 2359300
  219.2 1.0 copy-start.2
  220.2 4.5 %copy-start.6 = (pred[1024,1024]{0,1:T(8,128)(4,1)S(1)}, pred[1024,1024]{0,1:T(8,128)(4,1)}, u32[]{:S(2)}) copy-start(pred[1024,1024]{0,1:T(8,128)(4,1)} %fusion.20) | copy-start | bytes 3145732
  252.8 8.7 %copy-start.10 = (s32[1024]{0:T(1024)S(1)}, s32[1024]{0:T(1024)}, u32[]{:S(2)}) copy-start(s32[1024]{0:T(1024)} %param.16) | copy-start | bytes 12292
  255.4 34.6 %all-to-all-start.1 = ((bf16[64,16,512]{2,1,0:T(8,128)(2,1)}), bf16[64,16,512]{2,1,0:T(8,128)(2,1)S(1)}, u32[]{:S(2)}, u32[]{:S(2)}) async-start(bf16[64,16,512]{2,1,0:T(8,128)(2,1)} %bitcast.40), calls=%async_computation.1 | async-start | bytes 2097152 | tf_op jit(solution)/shard_map/all_to_all | solution.py:129
  336.2 14.1 %copy-start.3 = (bf16[1024,512]{1,0:T(8,128)(2,1)S(1)}, bf16[1024,512]{1,0:T(8,128)(2,1)}, u32[]{:S(2)}) copy-start(bf16[1024,512]{1,0:T(8,128)(2,1)} %gather_fusion.3) | copy-start | bytes 3145732
Sparse Core Ops, SparseCore 0:
  247.8 46.0 reduce-scatter.1
